TPU v7x, 32 devices: a whole 2x2x4 slice. The times are simulated.
32 devices in a mesh: dp: 4 (over z), seq: 2 (over x), tensor: 4 (over y, core).
Axes of the slice: x: 2, y: 2, z: 4, core: 2. Of those that a mesh axis runs over, the one named last changes fastest.
Arguments:
- inputs: bfloat16 [4, 4096, 768], P('dp', 'seq'), may hold values from -6 to 6
- pass_embed: float32 [768], replicated, may hold values from -3 to 3
- norm1_gain: float32 [768], replicated, may hold values from 0.5 to 1.5
- norm1_shift: float32 [768], replicated, may hold values from -1 to 1
- w_qkv: bfloat16 [3, 768, 768], P(None, None, 'tensor'), may hold values from -0.21875 to 0.21875
- b_qv: float32 [2, 768], P(None, 'tensor'), may hold values from -1 to 1
- w_out: bfloat16 [768, 768], P('tensor'), may hold values from -0.875 to 0.875
- b_out: float32 [768], replicated, may hold values from -1 to 1
- norm2_gain: float32 [768], replicated, may hold values from 0.5 to 1.5
- norm2_shift: float32 [768], replicated, may hold values from -1 to 1
- w_up: bfloat16 [768, 3072], P(None, 'tensor'), may hold values from -0.21875 to 0.21875
- b_up: float32 [3072], P('tensor'), may hold values from -1.5 to 1.5
- w_down: bfloat16 [3072, 768], P('tensor'), may hold values from -0.109375 to 0.109375
- b_down: float32 [768], replicated, may hold values from -1 to 1
- out_grad: bfloat16 [4, 4096, 768], P('dp', 'seq'), may hold values from -6 to 6
- seg_id: int32 [4, 4096], P('dp'), may hold values from 0 to 12, as said below
- parent: int32 [4, 13], P('dp'), may hold values from 0 to 4, as said below
Outputs:
- output: bfloat16 [4, 4096, 768], P('dp', ('seq', 'tensor'))
- input_grad: bfloat16 [4, 4096, 768], P('dp', ('seq', 'tensor'))
- grad_pass: float32 [768], replicated
- grad_norm1_gain: float32 [768], replicated
- grad_norm1_shift: float32 [768], replicated
- grad_w_qkv: float32 [3, 768, 768], P(None, None, 'tensor')
- grad_b_qv: float32 [2, 768], P(None, 'tensor')
- grad_w_out: float32 [768, 768], P('tensor')
- grad_b_out: float32 [768], replicated
- grad_norm2_gain: float32 [768], replicated
- grad_norm2_shift: float32 [768], replicated
- grad_w_up: float32 [768, 3072], P(None, 'tensor')
- grad_b_up: float32 [3072], P('tensor')
- grad_w_down: float32 [3072, 768], P('tensor')
- grad_b_down: float32 [768], replicated
Inputs may be any that keep to these rules, and one draw needn't show every extreme that they name: `seg_id`: in each tree segment 0 (the trunk) covers 1024 consecutive tokens starting at a multiple of 1024; each other segment covers 256 consecutive tokens starting at a multiple of 256. Segment 0 is its own parent; segments 1 to 4 have parent 0; each of them is the parent of exactly two of the other segments.
All inputs are finite; a program needn't handle non-finite values.
Results may differ from a plain program's by a relative error of at most 0.019.
Values may be sent and summed in bfloat16 or wider, within the bound.
No kernel may reach another device: no remote copies, remote signals or barrier semaphores. Data moves between devices by JAX's collectives and lax.ppermute only.
A program may use at most 256 MiB of HBM per device.

v0:
```python
import jax
import jax.numpy as jnp
from jax import lax
from jax.sharding import PartitionSpec as P

HD = 64
EPS = 1e-05
ROOT = 0.7978845608028654


def norm_stats(values):
    row_mean = jnp.mean(values, -1, keepdims=True)
    centred = values - row_mean
    inv_std = lax.rsqrt(jnp.mean(centred * centred, -1, keepdims=True) + EPS)
    return (centred * inv_std, inv_std)


def norm_back(grad_out, normal, inv_std, gain_vec):
    scaled = grad_out * gain_vec
    return inv_std * (
        scaled
        - jnp.mean(scaled, -1, keepdims=True)
        - normal * jnp.mean(scaled * normal, -1, keepdims=True)
    )


def gelu_parts(pre_act):
    cubic_term = 0.044715 * pre_act * pre_act * pre_act
    tangent = jnp.tanh(ROOT * (pre_act + cubic_term))
    gelu_value = 0.5 * pre_act * (1.0 + tangent)
    gelu_slope = 0.5 * (1.0 + tangent) + 0.5 * pre_act * (1.0 - tangent * tangent) * ROOT * (
        1.0 + 3.0 * 0.044715 * pre_act * pre_act
    )
    return (gelu_value, gelu_slope)


def forward_rows(left, right):
    return jnp.einsum("tbd,de->tbe", left, right, preferred_element_type=jnp.float32)


def weight_grad(left, right):
    return jnp.einsum("tbd,tbe->de", left, right, preferred_element_type=jnp.float32)


def input_rows(grad_rows, weight):
    return jnp.einsum("tbe,de->tbd", grad_rows, weight, preferred_element_type=jnp.float32)


def row_total(values):
    return jnp.sum(values.astype(jnp.float32), axis=(0, 1))


def ancestry(parent_row):
    labels = jnp.arange(parent_row.shape[0], dtype=jnp.int32)
    step_up = (
        (parent_row[:, None] == labels[None, :]) & (labels[:, None] != labels[None, :])
    ).astype(jnp.float32)
    return step_up + jnp.dot(step_up, step_up)


def visibility(seg_query, pos_query, seg_keys, ancestor):
    labels = jnp.arange(ancestor.shape[0], dtype=jnp.int32)
    query_hot = (seg_query[:, None] == labels[None, :]).astype(jnp.float32)
    key_hot = (labels[:, None] == seg_keys[None, :]).astype(jnp.float32)
    reachable = jnp.dot(jnp.dot(query_hot, ancestor), key_hot)
    key_pos = jnp.arange(seg_keys.shape[0], dtype=jnp.int32)
    same_seg = (seg_query[:, None] == seg_keys[None, :]) & (pos_query[:, None] >= key_pos[None, :])
    return same_seg | (reachable > 0.5)


def attend(queries, key_heads, value_heads, seg_row, ancestor, first_row):
    block_len = queries.shape[0]
    head_count = key_heads.shape[1]
    blk_width = min(512, block_len)
    blk_count = block_len // blk_width
    q_blocks = queries.reshape(blk_count, blk_width, head_count, HD)
    starts = first_row + blk_width * jnp.arange(blk_count, dtype=jnp.int32)

    def one_block(pieces):
        q_block, blk_start = pieces
        visible = visibility(
            lax.dynamic_slice_in_dim(seg_row, blk_start, blk_width),
            blk_start + jnp.arange(blk_width, dtype=jnp.int32),
            seg_row,
            ancestor,
        )
        scores = (
            jnp.einsum("qhd,khd->hqk", q_block, key_heads, preferred_element_type=jnp.float32)
            * 0.125
        )
        scores = jnp.where(visible[None], scores, -jnp.inf)
        row_top = jnp.max(scores, -1, keepdims=True)
        weights = jnp.exp(scores - row_top)
        row_sum = jnp.sum(weights, -1, keepdims=True)
        prob_low = (weights / row_sum).astype(jnp.bfloat16)
        mixture = jnp.einsum(
            "hqk,khd->qhd", prob_low, value_heads, preferred_element_type=jnp.float32
        )
        return (mixture, (row_top + jnp.log(row_sum))[..., 0])

    mixture, log_sums = lax.map(one_block, (q_blocks, starts))
    return (mixture.reshape(block_len, head_count * HD), log_sums)


def attend_back(queries, key_heads, value_heads, grad_mix, log_sums, seg_row, ancestor, first_row):
    block_len = queries.shape[0]
    head_count = key_heads.shape[1]
    blk_width = min(512, block_len)
    blk_count = block_len // blk_width
    q_blocks = queries.reshape(blk_count, blk_width, head_count, HD)
    g_blocks = grad_mix.reshape(blk_count, blk_width, head_count, HD)
    starts = first_row + blk_width * jnp.arange(blk_count, dtype=jnp.int32)

    def one_block(totals, pieces):
        q_block, g_block, lse_block, blk_start = pieces
        visible = visibility(
            lax.dynamic_slice_in_dim(seg_row, blk_start, blk_width),
            blk_start + jnp.arange(blk_width, dtype=jnp.int32),
            seg_row,
            ancestor,
        )
        scores = (
            jnp.einsum("qhd,khd->hqk", q_block, key_heads, preferred_element_type=jnp.float32)
            * 0.125
        )
        probs_full = jnp.where(visible[None], jnp.exp(scores - lse_block[..., None]), 0.0)
        grad_prob = jnp.einsum(
            "qhd,khd->hqk", g_block, value_heads, preferred_element_type=jnp.float32
        )
        inner = jnp.sum(probs_full * grad_prob, -1, keepdims=True)
        grad_score = (probs_full * (grad_prob - inner)).astype(jnp.bfloat16)
        grad_query = (
            jnp.einsum("hqk,khd->qhd", grad_score, key_heads, preferred_element_type=jnp.float32)
            * 0.125
        )
        key_sum = (
            totals[0]
            + jnp.einsum("hqk,qhd->khd", grad_score, q_block, preferred_element_type=jnp.float32)
            * 0.125
        )
        value_sum = totals[1] + jnp.einsum(
            "hqk,qhd->khd",
            probs_full.astype(jnp.bfloat16),
            g_block,
            preferred_element_type=jnp.float32,
        )
        totals = (key_sum, value_sum)
        return (totals, (grad_query, inner[..., 0]))

    zero_keys = jnp.zeros(key_heads.shape, jnp.float32)
    start_totals = (zero_keys, zero_keys)
    totals, (grad_query, inner) = lax.scan(
        one_block, start_totals, (q_blocks, g_blocks, log_sums, starts)
    )
    length = key_heads.shape[0]
    kv_term = None
    kv_term = jnp.concatenate(
        [totals[0].reshape(length, head_count * HD), totals[1].reshape(length, head_count * HD)], -1
    )
    return (grad_query.reshape(block_len, head_count * HD), inner, kv_term)


def local(
    inputs,
    pass_embed,
    norm1_gain,
    norm1_shift,
    w_qkv,
    b_qv,
    w_out,
    b_out,
    norm2_gain,
    norm2_shift,
    w_up,
    b_up,
    w_down,
    b_down,
    out_grad,
    seg_id,
    parent,
):
    tree_count = inputs.shape[0]
    block_len = inputs.shape[1]
    local_width = w_qkv.shape[2]
    head_count = local_width // HD
    sub_len = block_len // lax.axis_size("tensor")
    sub_start = lax.axis_index("tensor") * sub_len
    first_row = lax.axis_index("seq") * block_len

    def own_rows(values):
        return lax.dynamic_slice_in_dim(values, sub_start, sub_len, 1)

    residual = inputs.astype(jnp.float32) + pass_embed
    norm_one, inv_one = norm_stats(residual)
    normed = (norm_one * norm1_gain + norm1_shift).astype(jnp.bfloat16)
    queries = (forward_rows(normed, w_qkv[0]) + b_qv[0]).astype(jnp.bfloat16)
    key_loc = forward_rows(normed, w_qkv[1]).astype(jnp.bfloat16)
    value_loc = (forward_rows(normed, w_qkv[2]) + b_qv[1]).astype(jnp.bfloat16)
    gathered = lax.all_gather(jnp.concatenate([key_loc, value_loc], -1), "seq", axis=1, tiled=True)
    length = gathered.shape[1]
    key_all = gathered[..., :local_width].reshape(tree_count, length, head_count, HD)
    value_all = gathered[..., local_width:].reshape(tree_count, length, head_count, HD)
    ancestors = [ancestry(parent[0])]
    tree_idx = 0
    mixed_tree, log_sums = attend(
        queries[tree_idx],
        key_all[tree_idx],
        value_all[tree_idx],
        seg_id[tree_idx],
        ancestors[tree_idx],
        first_row,
    )
    mix_list = [mixed_tree]
    lse_list = [log_sums]
    mixture = jnp.stack(mix_list).astype(jnp.bfloat16)
    partial_attn = forward_rows(mixture, w_out)
    middle = (
        residual + lax.psum(partial_attn.astype(jnp.bfloat16), "tensor").astype(jnp.float32) + b_out
    )
    norm_two, inv_two = norm_stats(middle)
    lifted_own = (norm_two * norm2_gain + norm2_shift).astype(jnp.bfloat16)
    pre_act = forward_rows(lifted_own, w_up) + b_up
    gelu_value, gelu_slope = gelu_parts(pre_act)
    active = gelu_value.astype(jnp.bfloat16)
    partial_mlp = forward_rows(active, w_down)
    output = own_rows(
        middle + lax.psum(partial_mlp.astype(jnp.bfloat16), "tensor").astype(jnp.float32) + b_down
    ).astype(jnp.bfloat16)
    grad_w_down = weight_grad(active, out_grad)
    grad_b_down = row_total(out_grad)
    grad_pre = (input_rows(out_grad, w_down) * gelu_slope).astype(jnp.bfloat16)
    grad_w_up = weight_grad(lifted_own, grad_pre)
    grad_b_up = row_total(grad_pre)
    partial_lift = input_rows(grad_pre, w_up)
    grad_lift = lax.psum(partial_lift.astype(jnp.bfloat16), "tensor").astype(jnp.float32)
    grad_middle = out_grad.astype(jnp.float32) + norm_back(grad_lift, norm_two, inv_two, norm2_gain)
    grad_g2 = row_total(grad_lift * norm_two)
    grad_b2 = row_total(grad_lift)
    grad_b_out = row_total(grad_middle)
    proj_low = grad_middle.astype(jnp.bfloat16)
    grad_w_out = weight_grad(mixture, proj_low)
    grad_mix = input_rows(proj_low, w_out).astype(jnp.bfloat16)
    tree_idx = 0
    grad_query, inner, kv_term = attend_back(
        queries[tree_idx],
        key_all[tree_idx],
        value_all[tree_idx],
        grad_mix[tree_idx],
        lse_list[tree_idx],
        seg_id[tree_idx],
        ancestors[tree_idx],
        first_row,
    )
    query_list = [grad_query]
    term_list = [kv_term]
    kv_grads = lax.psum_scatter(
        jnp.stack(term_list).astype(jnp.bfloat16), "seq", scatter_dimension=1, tiled=True
    ).astype(jnp.float32)
    grad_q = jnp.stack(query_list).astype(jnp.bfloat16)
    grad_k = kv_grads[..., :local_width].astype(jnp.bfloat16)
    grad_v = kv_grads[..., local_width:].astype(jnp.bfloat16)
    grad_w_qkv = jnp.stack(
        [weight_grad(normed, grad_q), weight_grad(normed, grad_k), weight_grad(normed, grad_v)]
    )
    grad_b_qv = jnp.stack([row_total(grad_q), row_total(grad_v)])
    partial_norm = (
        input_rows(grad_q, w_qkv[0]) + input_rows(grad_k, w_qkv[1]) + input_rows(grad_v, w_qkv[2])
    )
    grad_norm = lax.psum(partial_norm.astype(jnp.bfloat16), "tensor").astype(jnp.float32)
    grad_resid = grad_middle + norm_back(grad_norm, norm_one, inv_one, norm1_gain)
    input_grad = own_rows(grad_resid).astype(jnp.bfloat16)
    grad_pass = row_total(grad_resid)
    grad_g1 = row_total(grad_norm * norm_one)
    grad_b1 = row_total(grad_norm)
    summed = lax.psum(
        (
            grad_w_qkv,
            grad_b_qv,
            grad_w_out,
            grad_w_up,
            grad_b_up,
            grad_w_down,
            grad_b_down,
            grad_pass,
            grad_g1,
            grad_b1,
            grad_g2,
            grad_b2,
            grad_b_out,
        ),
        ("dp", "seq"),
    )
    return (
        output,
        input_grad,
        summed[7],
        summed[8],
        summed[9],
        summed[0],
        summed[1],
        summed[2],
        summed[12],
        summed[10],
        summed[11],
        summed[3],
        summed[4],
        summed[5],
        summed[6],
    )


def solution(mesh):
    return jax.shard_map(
        local,
        mesh=mesh,
        in_specs=(
            P("dp", "seq", None),
            P(),
            P(),
            P(),
            P(None, None, "tensor"),
            P(None, "tensor"),
            P("tensor", None),
            P(),
            P(),
            P(),
            P(None, "tensor"),
            P("tensor"),
            P("tensor", None),
            P(),
            P("dp", "seq", None),
            P("dp", None),
            P("dp", None),
        ),
        out_specs=(
            P("dp", ("seq", "tensor"), None),
            P("dp", ("seq", "tensor"), None),
            P(),
            P(),
            P(),
            P(None, None, "tensor"),
            P(None, "tensor"),
            P("tensor", None),
            P(),
            P(),
            P(),
            P(None, "tensor"),
            P("tensor"),
            P("tensor", None),
            P(),
        ),
        check_vma=False,
    )
```

profile of v0, /device:TPU:0, one launch (start us, length us, event | category | flops | bytes accessed | tf_op | source)
XLA Modules:
  0.0 1257.9 jit_solution(2198636816615368359)
XLA Ops:
  23.9 43.7 %all-gather.2.cloned.1.call-done = bf16[1,4096,384]{1,2,0:T(8,128)(2,1)} async-done(((bf16[1,2048,384]{1,2,0:T(8,128)(2,1)}), bf16[1,4096,384]{1,2,0:T(8,128)(2,1)}) %all-gather.2.cloned.1.call-update) | async-done | bytes 3145744 | tf_op jit(solution)/shard_map/all_gather | solution.py:199
  71.8 184.3 %while.27 = (s32[]{:T(128)}, bf16[4,512,3,64]{1,3,2,0:T(8,128)(2,1)}, f32[4,3,512]{2,1,0:T(4,128)}, s32[4]{0:T(128)S(1)}, s32[4096]{0:T(1024)}, /*index=5*/s32[1...) while((s32[]{:T(128)}, ...), condition=%wide.region_5.6_spmd, body=%wide.region_2.5_spmd.sunk | while | flops 1751353856 | bytes 108675712 | solution.py:101
  105.2 12.1 fusion.193
  127.1 12.1 fusion.191
  151.2 12.1 fusion.193
  173.1 12.1 fusion.191
  197.1 12.1 fusion.193
  219.0 12.1 fusion.191
  243.1 12.1 fusion.193
  262.8 68.4 %all-reduce.8.cloned.1.call-done = bf16[1,2048,768]{2,1,0:T(8,128)(2,1)} async-done(((bf16[1,2048,768]{2,1,0:T(8,128)(2,1)}), bf16[1,2048,768]{2,1,0:T(8,128)(2,1)}) %all-reduce.8.cloned.1.call-update) | async-done | bytes 3145744 | tf_op jit(solution)/shard_map/psum | solution.py:218
  353.9 68.6 %all-reduce.10.cloned.1.call-done = bf16[1,2048,768]{2,1,0:T(8,128)(2,1)} async-done(((bf16[1,2048,768]{2,1,0:T(8,128)(2,1)}), bf16[1,2048,768]{2,1,0:T(8,128)(2,1)}) %all-reduce.10.cloned.1.call-update) | async-done | bytes 3145744 | tf_op jit(solution)/shard_map/psum | solution.py:235
  445.2 377.5 %while.28 = (s32[]{:T(128)}, f32[4096,3,64]{0,2,1:T(8,128)}, f32[4096,3,64]{0,2,1:T(8,128)}, bf16[4,512,3,64]{1,3,2,0:T(8,128)(2,1)}, bf16[4,512,3,64]{1,3,2,0:T...) while((s32[]{:T(128)}, f32[4096,3,64]{0,2,1:T(8,128)}, ...), condition=%wide.region_15.16_spmd.clone, body=%wide.region_13.15_spmd.clone.sunk | while | flops 4190177792 | bytes 234558224 | solution.py:152
  453.9 13.3 %fusion.205 = f32[3,512,4096]{2,1,0:T(8,128)} fusion(bf16[4096,3,64]{0,2,1:T(8,128)(2,1)} %copy-done.1, bf16[4,512,3,64]{1,3,2,0:T(8,128)(2,1)} %copy-done.15, s32[]{:T(128)S(6)} %copy.60), kind=kOutput, calls=%fused_computation.48.clone.1 | convolution fusion | flops 805306368 | bytes 26935300 | tf_op jit(solution)/shard_map/while/body/eval_jaxpr/qhd,khd->hqk/dot_general | solution.py:123
  467.2 12.5 fusion.208
  479.8 18.3 %multiply_reduce_fusion.4 = (f32[3,512]{1,0:T(4,128)S(1)}, f32[3,512,4096]{2,1,0:T(8,128)}) fusion(f32[3,512,4096]{2,1,0:T(8,128)} %fusion.205, f32[3,512]{1,0:T(4,128)S(1)} %dynamic-slice_bitcast_fusion.2, pred[512,4096]{1,0:T(8,128)(4,1)S(1)} %fusion.206, bf16[4096,3,64]{0,2,1:T(8,128)(2,1)} %get-tuple-element.551, ...), kind=kOutput, calls=%fused_computation.25.clone.1 | convolution fusion | flops 836762112 | bytes 54210564 | tf_op jit(solution)/shard_map/while/body/eval_jaxpr/qhd,khd->hqk/dot_general | solution.py:127
  498.1 21.9 %multiply_convert_fusion.5 = bf16[3,512,4096]{2,1,0:T(8,128)(2,1)} fusion(f32[3,512,4096]{2,1,0:T(8,128)} %get-tuple-element.466, f32[3,512,4096]{2,1,0:T(8,128)} %fusion.205, f32[3,512]{1,0:T(4,128)S(1)} %get-tuple-element.467, f32[3,512]{1,0:T(4,128)S(1)} %dynamic-slice_bitcast_fusion.2, pred[512,4096]{1,0:T(8,128)(4,1)S(1)} %fusion.206), kind=kLoop, calls=%fused_computation.24.clone.1 | loop fusion | flops 37748736 | bytes 65024000 | tf_op jit(solution)/shard_map/while/body/eval_jaxpr/convert_element_type | solution.py:131
  546.7 13.3 %fusion.205 = f32[3,512,4096]{2,1,0:T(8,128)} fusion(bf16[4096,3,64]{0,2,1:T(8,128)(2,1)} %copy-done.1, bf16[4,512,3,64]{1,3,2,0:T(8,128)(2,1)} %copy-done.15, s32[]{:T(128)S(6)} %copy.60), kind=kOutput, calls=%fused_computation.48.clone.1 | convolution fusion | flops 805306368 | bytes 26935300 | tf_op jit(solution)/shard_map/while/body/eval_jaxpr/qhd,khd->hqk/dot_general | solution.py:123
  560.0 13.6 %fusion.208 = f32[4096,3,64]{0,2,1:T(8,128)} fusion(f32[3,512,4096]{2,1,0:T(8,128)} %fusion.205, f32[3,512]{1,0:T(4,128)S(1)} %dynamic-slice_bitcast_fusion.2, pred[512,4096]{1,0:T(8,128)(4,1)S(1)} %fusion.206, f32[4096,3,64]{0,2,1:T(8,128)} %get-tuple-element.525, pred[]{:T(512)S(6)} %compare.3, bf16[4,512,3,64]{1,3,2,0:T(8,128)(2,1)} %get-tuple-element.550, ...), kind=kOutput, calls=%fused_computation.37.clone.1 | convolution fusion | flops 832045056 | bytes 33757188 | tf_op jit(solution)/shard_map/while/body/eval_jaxpr/hqk,qhd->khd/dot_general | solution.py:141
  573.6 18.3 %multiply_reduce_fusion.4 = (f32[3,512]{1,0:T(4,128)S(1)}, f32[3,512,4096]{2,1,0:T(8,128)}) fusion(f32[3,512,4096]{2,1,0:T(8,128)} %fusion.205, f32[3,512]{1,0:T(4,128)S(1)} %dynamic-slice_bitcast_fusion.2, pred[512,4096]{1,0:T(8,128)(4,1)S(1)} %fusion.206, bf16[4096,3,64]{0,2,1:T(8,128)(2,1)} %get-tuple-element.551, ...), kind=kOutput, calls=%fused_computation.25.clone.1 | convolution fusion | flops 836762112 | bytes 54210564 | tf_op jit(solution)/shard_map/while/body/eval_jaxpr/qhd,khd->hqk/dot_general | solution.py:127
  591.9 21.9 %multiply_convert_fusion.5 = bf16[3,512,4096]{2,1,0:T(8,128)(2,1)} fusion(f32[3,512,4096]{2,1,0:T(8,128)} %get-tuple-element.466, f32[3,512,4096]{2,1,0:T(8,128)} %fusion.205, f32[3,512]{1,0:T(4,128)S(1)} %get-tuple-element.467, f32[3,512]{1,0:T(4,128)S(1)} %dynamic-slice_bitcast_fusion.2, pred[512,4096]{1,0:T(8,128)(4,1)S(1)} %fusion.206), kind=kLoop, calls=%fused_computation.24.clone.1 | loop fusion | flops 37748736 | bytes 65024000 | tf_op jit(solution)/shard_map/while/body/eval_jaxpr/convert_element_type | solution.py:131
  641.5 13.3 %fusion.205 = f32[3,512,4096]{2,1,0:T(8,128)} fusion(bf16[4096,3,64]{0,2,1:T(8,128)(2,1)} %copy-done.1, bf16[4,512,3,64]{1,3,2,0:T(8,128)(2,1)} %copy-done.15, s32[]{:T(128)S(6)} %copy.60), kind=kOutput, calls=%fused_computation.48.clone.1 | convolution fusion | flops 805306368 | bytes 26935300 | tf_op jit(solution)/shard_map/while/body/eval_jaxpr/qhd,khd->hqk/dot_general | solution.py:123
  654.7 13.6 %fusion.208 = f32[4096,3,64]{0,2,1:T(8,128)} fusion(f32[3,512,4096]{2,1,0:T(8,128)} %fusion.205, f32[3,512]{1,0:T(4,128)S(1)} %dynamic-slice_bitcast_fusion.2, pred[512,4096]{1,0:T(8,128)(4,1)S(1)} %fusion.206, f32[4096,3,64]{0,2,1:T(8,128)} %get-tuple-element.525, pred[]{:T(512)S(6)} %compare.3, bf16[4,512,3,64]{1,3,2,0:T(8,128)(2,1)} %get-tuple-element.550, ...), kind=kOutput, calls=%fused_computation.37.clone.1 | convolution fusion | flops 832045056 | bytes 33757188 | tf_op jit(solution)/shard_map/while/body/eval_jaxpr/hqk,qhd->khd/dot_general | solution.py:141
  668.4 18.3 %multiply_reduce_fusion.4 = (f32[3,512]{1,0:T(4,128)S(1)}, f32[3,512,4096]{2,1,0:T(8,128)}) fusion(f32[3,512,4096]{2,1,0:T(8,128)} %fusion.205, f32[3,512]{1,0:T(4,128)S(1)} %dynamic-slice_bitcast_fusion.2, pred[512,4096]{1,0:T(8,128)(4,1)S(1)} %fusion.206, bf16[4096,3,64]{0,2,1:T(8,128)(2,1)} %get-tuple-element.551, ...), kind=kOutput, calls=%fused_computation.25.clone.1 | convolution fusion | flops 836762112 | bytes 54210564 | tf_op jit(solution)/shard_map/while/body/eval_jaxpr/qhd,khd->hqk/dot_general | solution.py:127
  686.7 21.9 %multiply_convert_fusion.5 = bf16[3,512,4096]{2,1,0:T(8,128)(2,1)} fusion(f32[3,512,4096]{2,1,0:T(8,128)} %get-tuple-element.466, f32[3,512,4096]{2,1,0:T(8,128)} %fusion.205, f32[3,512]{1,0:T(4,128)S(1)} %get-tuple-element.467, f32[3,512]{1,0:T(4,128)S(1)} %dynamic-slice_bitcast_fusion.2, pred[512,4096]{1,0:T(8,128)(4,1)S(1)} %fusion.206), kind=kLoop, calls=%fused_computation.24.clone.1 | loop fusion | flops 37748736 | bytes 65024000 | tf_op jit(solution)/shard_map/while/body/eval_jaxpr/convert_element_type | solution.py:131
  736.2 13.3 %fusion.205 = f32[3,512,4096]{2,1,0:T(8,128)} fusion(bf16[4096,3,64]{0,2,1:T(8,128)(2,1)} %copy-done.1, bf16[4,512,3,64]{1,3,2,0:T(8,128)(2,1)} %copy-done.15, s32[]{:T(128)S(6)} %copy.60), kind=kOutput, calls=%fused_computation.48.clone.1 | convolution fusion | flops 805306368 | bytes 26935300 | tf_op jit(solution)/shard_map/while/body/eval_jaxpr/qhd,khd->hqk/dot_general | solution.py:123
  749.5 13.6 %fusion.208 = f32[4096,3,64]{0,2,1:T(8,128)} fusion(f32[3,512,4096]{2,1,0:T(8,128)} %fusion.205, f32[3,512]{1,0:T(4,128)S(1)} %dynamic-slice_bitcast_fusion.2, pred[512,4096]{1,0:T(8,128)(4,1)S(1)} %fusion.206, f32[4096,3,64]{0,2,1:T(8,128)} %get-tuple-element.525, pred[]{:T(512)S(6)} %compare.3, bf16[4,512,3,64]{1,3,2,0:T(8,128)(2,1)} %get-tuple-element.550, ...), kind=kOutput, calls=%fused_computation.37.clone.1 | convolution fusion | flops 832045056 | bytes 33757188 | tf_op jit(solution)/shard_map/while/body/eval_jaxpr/hqk,qhd->khd/dot_general | solution.py:141
  763.1 18.3 %multiply_reduce_fusion.4 = (f32[3,512]{1,0:T(4,128)S(1)}, f32[3,512,4096]{2,1,0:T(8,128)}) fusion(f32[3,512,4096]{2,1,0:T(8,128)} %fusion.205, f32[3,512]{1,0:T(4,128)S(1)} %dynamic-slice_bitcast_fusion.2, pred[512,4096]{1,0:T(8,128)(4,1)S(1)} %fusion.206, bf16[4096,3,64]{0,2,1:T(8,128)(2,1)} %get-tuple-element.551, ...), kind=kOutput, calls=%fused_computation.25.clone.1 | convolution fusion | flops 836762112 | bytes 54210564 | tf_op jit(solution)/shard_map/while/body/eval_jaxpr/qhd,khd->hqk/dot_general | solution.py:127
  781.4 21.9 %multiply_convert_fusion.5 = bf16[3,512,4096]{2,1,0:T(8,128)(2,1)} fusion(f32[3,512,4096]{2,1,0:T(8,128)} %get-tuple-element.466, f32[3,512,4096]{2,1,0:T(8,128)} %fusion.205, f32[3,512]{1,0:T(4,128)S(1)} %get-tuple-element.467, f32[3,512]{1,0:T(4,128)S(1)} %dynamic-slice_bitcast_fusion.2, pred[512,4096]{1,0:T(8,128)(4,1)S(1)} %fusion.206), kind=kLoop, calls=%fused_computation.24.clone.1 | loop fusion | flops 37748736 | bytes 65024000 | tf_op jit(solution)/shard_map/while/body/eval_jaxpr/convert_element_type | solution.py:131
  843.1 29.5 %reduce-scatter.2.cloned.1.call-done = bf16[1,2048,384]{1,2,0:T(8,128)(2,1)} async-done(((bf16[1,4096,384]{1,2,0:T(8,128)(2,1)}), bf16[1,2048,384]{1,2,0:T(8,128)(2,1)}) %reduce-scatter.2.cloned.1.call-update) | async-done | bytes 1572880 | tf_op jit(solution)/shard_map/reduce_scatter | solution.py:256
  902.4 97.5 %all-reduce.14.cloned.1.call-done = (bf16[1,2048,768]{2,1,0:T(8,128)(2,1)}, bf16[1,2048,768]{2,1,0:T(8,128)(2,1)}) async-done(((bf16[1,2048,768]{2,1,0:T(8,128)(2,1)}, bf16[1,2048,768]{2,1,0:T(8,128)(2,1)}), (bf16[1,2048,768]{2,1,0:T(8,128)(2,1)}, bf16[1,2048,768]{2,1,0:T(8,128)(2,1)})) %all-reduce.14.cloned.1.call-update) | async-done | bytes 6291472 | tf_op jit(solution)/shard_map/psum | solution.py:227
  1011.9 41.2 %all-reduce = (f32[768]{0:T(1024)}, f32[768]{0:T(1024)}, f32[768]{0:T(1024)}, f32[2,192]{1,0:T(2,128)}, f32[768]{0:T(1024)}, /*index=5*/f32[768]{0:T(1024)}, f32[768]{0:T(1024)}, f32[768]{0:T(1024)}, f32[768]{0:T(1024)}) all-reduce(f32[768]{0:T(1024)S(1)} %get-tuple-element.301, ...), channel_id=1, replica_groups=mesh['dp'=4,'seq'=2,'tensor'=4] {'dp','seq'}, use_global_device_ids=true, to_apply=%region_21.22 | all-reduce | flops 6528 | bytes 52224 | tf_op jit(solution)/shard_map/psum | solution.py:275
  1058.1 185.1 %all-reduce.12.cloned.1.call-done = (f32[3,768,192]{1,2,0:T(8,128)}, f32[192,768]{1,0:T(8,128)}, f32[768,768]{1,0:T(8,128)}, f32[768,768]{1,0:T(8,128)}) async-done(((f32[3,768,192]{1,2,0:T(8,128)}, f32[192,768]{1,0:T(8,128)}, f32[768,768]{1,0:T(8,128)}, f32[768,768]{1,0:T(8,128)}), (f32[3,768,192]{1,2,0:T(8,128)}, f32[192,768]{1,0:T(8,128)}, f32[768,768]{1,0:T(8,128)}, ...) | async-done | bytes 7077904 | tf_op jit(solution)/shard_map/psum | solution.py:275
  (313 shorter events, 339.9 us)
Async XLA Ops:
  7.2 334.1 %copy-start = (bf16[768,768]{1,0:T(8,128)(2,1)S(1)}, bf16[768,768]{1,0:T(8,128)(2,1)}, u32[]{:S(2)}) copy-start(bf16[768,768]{1,0:T(8,128)(2,1)} %param.33) | copy-start | bytes 3538948
  7.2 60.3 %all-gather.2.cloned.1.call-start = ((), (), s32[]{:S(2)}) async-start(), calls=%async_computation.1 | async-start | bytes 4718592 | tf_op jit(solution)/shard_map/all_gather | solution.py:199
  19.8 311.5 %all-reduce.8.cloned.1.call-start = ((), (), s32[]{:S(2)}) async-start(), calls=%async_computation.2 | async-start | bytes 6291456 | tf_op jit(solution)/shard_map/psum | solution.py:218
  81.1 12.1 copy-start.8
  93.2 12.0 copy-start.7
  93.2 12.0 copy-start.24
  127.1 12.1 copy-start.8
  139.2 12.0 copy-start.7
  139.2 12.0 copy-start.24
  173.1 12.1 copy-start.8
  185.1 12.0 copy-start.7
  185.1 12.0 copy-start.24
  219.0 12.1 copy-start.8
  231.1 12.0 copy-start.7
  231.1 12.0 copy-start.24
  256.1 79.3 %copy-start.55 = (s32[4]{0:T(128)}, s32[4]{0:T(128)S(1)}, u32[]{:S(2)}) copy-start(s32[4]{0:T(128)S(1)} %get-tuple-element.618) | copy-start | bytes 52
  256.1 79.3 %copy-start.58 = (bf16[13,13]{1,0:T(8,128)(2,1)}, bf16[13,13]{1,0:T(8,128)(2,1)S(1)}, u32[]{:S(2)}) copy-start(bf16[13,13]{1,0:T(8,128)(2,1)S(1)} %get-tuple-element.636) | copy-start | bytes 1018
  256.1 75.2 %copy-start.34 = (f32[768]{0:T(1024)S(1)}, f32[768]{0:T(1024)}, u32[]{:S(2)}) copy-start(f32[768]{0:T(1024)} %param.22) | copy-start | bytes 9220
  256.1 75.2 %copy-start.46 = (f32[768]{0:T(1024)S(1)}, f32[768]{0:T(1024)}, u32[]{:S(2)}) copy-start(f32[768]{0:T(1024)} %param.28) | copy-start | bytes 9220
  262.6 159.9 %all-reduce.10.cloned.1.call-start = ((), (), s32[]{:S(2)}) async-start(), calls=%async_computation.3 | async-start | bytes 6291456 | tf_op jit(solution)/shard_map/psum | solution.py:235
  353.8 518.8 %reduce-scatter.2.cloned.1.call-start = ((), (), s32[]{:S(2)}) async-start(), calls=%async_computation.4 | async-start | bytes 4718592 | tf_op jit(solution)/shard_map/reduce_scatter | solution.py:256
  434.5 10.8 copy-start.56
  520.0 9.7 copy-start.16
  708.6 9.7 copy-start.16
  829.0 170.9 %all-reduce.14.cloned.1.call-start = ((), (), s32[]{:S(2)}) async-start(), calls=%async_computation.6 | async-start | bytes 12582912 | tf_op jit(solution)/shard_map/psum | solution.py:227
  879.9 363.2 %all-reduce.12.cloned.1.call-start = ((), (), s32[]{:S(2)}) async-start(), calls=%async_computation.5 | async-start | bytes 14155776 | tf_op jit(solution)/shard_map/psum | solution.py:275
  880.2 15.8 %slice-start = ((s8[6291456]{0:T(1024)(128)(4,1)}), s8[4194304]{0:T(1024)(128)(4,1)S(1)}, s32[]{:S(2)}) async-start(s8[6291456]{0:T(1024)(128)(4,1)} %bitcast.206), calls=%async_computation.7 | async-start | bytes 8388608
  899.3 100.6 %copy-start.32 = (f32[2048]{0:T(1024)S(1)}, f32[2048]{0:T(1024)}, u32[]{:S(2)}) copy-start(f32[2048]{0:T(1024)} %copy-done.31) | copy-start | bytes 24580
  899.3 100.6 %copy-start.35 = (f32[768]{0:T(1024)S(1)}, f32[768]{0:T(1024)}, u32[]{:S(2)}) copy-start(f32[768]{0:T(1024)} %param.22) | copy-start | bytes 9220
  899.3 100.6 %copy-start.41 = (f32[768]{0:T(1024)S(1)}, f32[768]{0:T(1024)}, u32[]{:S(2)}) copy-start(f32[768]{0:T(1024)} %param.23) | copy-start | bytes 9220
  901.4 103.8 %copy-start.37 = (f32[2048]{0:T(1024)S(1)}, f32[2048]{0:T(1024)}, u32[]{:S(2)}) copy-start(f32[2048]{0:T(1024)} %copy-done.36) | copy-start | bytes 24580
  1005.4 49.8 %copy-start.48 = (f32[768]{0:T(1024)S(1)}, f32[768]{0:T(1024)}, u32[]{:S(2)}) copy-start(f32[768]{0:T(1024)} %param.34) | copy-start | bytes 9220
  (64 other events, 343.6 us)
Sparse Core Ops, SparseCore 0:
  19.9 47.6 all-gather.1
  262.7 68.4 all-reduce.7
  353.9 68.5 all-reduce.9
  829.1 43.4 reduce-scatter.1
  880.1 119.7 all-reduce.13
  1005.9 237.1 all-reduce.11
where the time goes:
time: 1270 us; the launch traced here: 1260 us
  waiting for transfers between devices  493 us (39%)
  matrix products  449 us (35%)
  other arithmetic  193 us (15%)
  local copies, waits for them, and re-layouts  48.5 us (4%)
  blocking collectives  41.2 us (3%)
  loops' own time  17.1 us (1%)
  between operations  15 us (1%)
    psum x1, waiting for transfers between devices, local(): lax.psum((grad_w_qkv, grad_b_qv, grad_w_out, grad_w_up, grad_b_up, grad_w...  185 us
    dot_general x8, matrix products, one_block(): jnp.einsum('qhd,khd->hqk', q_block, key_heads, preferred_element_type=jnp...  101 us
    psum x1, waiting for transfers between devices, local(): lax.psum(partial_mlp.astype(jnp.bfloat16), 'tensor').astype(jnp.float32)  97.5 us
    convert_element_type x4, other arithmetic, one_block(): grad_score = (probs_full * (grad_prob - inner)).astype(jnp.bfloat16)  87.6 us
    dot_general x4, matrix products, one_block(): jnp.einsum('qhd,khd->hqk', g_block, value_heads, preferred_element_type=j...  73.2 us
    psum x1, waiting for transfers between devices, local(): lax.psum(partial_lift.astype(jnp.bfloat16), 'tensor').astype(jnp.float32)  68.6 us
    psum x1, waiting for transfers between devices, local(): lax.psum(partial_attn.astype(jnp.bfloat16), 'tensor').astype(jnp.float32)  68.4 us
    dot_general x4, matrix products, one_block(): jnp.einsum('hqk,qhd->khd', probs_full.astype(jnp.bfloat16), g_block, pref...  53.5 us
  transfers between devices with their start and end apart: 6, of which 6 were waited for; matrix products, arithmetic and copies ran while one was open for 5% of the time, Pallas kernels for 0%

commit v1 on v0

--- a/solution.py
+++ b/solution.py
@@ -2,6 +2,7 @@
 import jax.numpy as jnp
 from jax import lax
 from jax.sharding import PartitionSpec as P
+from jax.lax import psum
 
 HD = 64
 EPS = 1e-05
@@ -272,23 +273,26 @@
     grad_pass = row_total(grad_resid)
     grad_g1 = row_total(grad_norm * norm_one)
     grad_b1 = row_total(grad_norm)
-    summed = lax.psum(
-        (
-            grad_w_qkv,
-            grad_b_qv,
-            grad_w_out,
-            grad_w_up,
-            grad_b_up,
-            grad_w_down,
-            grad_b_down,
-            grad_pass,
-            grad_g1,
-            grad_b1,
-            grad_g2,
-            grad_b2,
-            grad_b_out,
+    summed = psum(
+        psum(
+            (
+                grad_w_qkv,
+                grad_b_qv,
+                grad_w_out,
+                grad_w_up,
+                grad_b_up,
+                grad_w_down,
+                grad_b_down,
+                grad_pass,
+                grad_g1,
+                grad_b1,
+                grad_g2,
+                grad_b2,
+                grad_b_out,
+            ),
+            axis_name="seq",
         ),
-        ("dp", "seq"),
+        axis_name="dp",
     )
     return (
         output,

time: 1270 us -> 1450 us (1.14)
  waiting for transfers between devices: 493 us -> 687 us
    psum x1 -> x2, waiting for transfers between devices: 185 us -> 361 us  [the longest x1 204 us: local(): psum(psum((grad_w_qkv, grad_b_qv, grad_w_out, grad_w_up, grad_b_up, grad_...]
    psum x1, waiting for transfers between devices: 97.5 us -> 120 us  [local(): lax.psum(partial_mlp.astype(jnp.bfloat16), 'tensor').astype(jnp.float32)]
    psum x1 -> x2, blocking collectives: 41.2 us -> 32.7 us  [the longest x1 24.2 us: local(): psum(psum((grad_w_qkv, grad_b_qv, grad_w_out, grad_w_up, grad_b_up, grad_...]
  transfers between devices with their start and end apart: 6 -> 7, of which waited for: 6 -> 7; matrix products, arithmetic and copies ran while one was open for 5% -> 4% of each run, Pallas kernels for 0% -> 0%
where the time goes in v1:
time: 1450 us; the launch traced here: 1440 us
  waiting for transfers between devices  687 us (47%)
  matrix products  448 us (31%)
  other arithmetic  194 us (13%)
  local copies, waits for them, and re-layouts  47.7 us (3%)
  blocking collectives  32.7 us (2%)
  loops' own time  17.1 us (1%)
  between operations  15.1 us (1%)
    psum x1, waiting for transfers between devices, local(): psum(psum((grad_w_qkv, grad_b_qv, grad_w_out, grad_w_up, grad_b_up, grad_...  204 us
    psum x1, waiting for transfers between devices, local(): psum((grad_w_qkv, grad_b_qv, grad_w_out, grad_w_up, grad_b_up, grad_w_dow...  157 us
    psum x1, waiting for transfers between devices, local(): lax.psum(partial_mlp.astype(jnp.bfloat16), 'tensor').astype(jnp.float32)  120 us
    dot_general x8, matrix products, one_block(): jnp.einsum('qhd,khd->hqk', q_block, key_heads, preferred_element_type=jnp...  101 us
    convert_element_type x4, other arithmetic, one_block(): grad_score = (probs_full * (grad_prob - inner)).astype(jnp.bfloat16)  87.6 us
    dot_general x4, matrix products, one_block(): jnp.einsum('qhd,khd->hqk', g_block, value_heads, preferred_element_type=j...  73.2 us
    psum x1, waiting for transfers between devices, local(): lax.psum(partial_lift.astype(jnp.bfloat16), 'tensor').astype(jnp.float32)  68.6 us
    psum x1, waiting for transfers between devices, local(): lax.psum(partial_attn.astype(jnp.bfloat16), 'tensor').astype(jnp.float32)  68.4 us
  transfers between devices with their start and end apart: 7, of which 7 were waited for; matrix products, arithmetic and copies ran while one was open for 4% of the time, Pallas kernels for 0%

profile of v1, /device:TPU:0, one launch (start us, length us, event | category | flops | bytes accessed | tf_op | source)
XLA Modules:
  0.0 1441.7 jit_solution(8261019158202671147)
XLA Ops:
  23.9 43.7 %all-gather.2.cloned.1.call-done = bf16[1,4096,384]{1,2,0:T(8,128)(2,1)} async-done(((bf16[1,2048,384]{1,2,0:T(8,128)(2,1)}), bf16[1,4096,384]{1,2,0:T(8,128)(2,1)}) %all-gather.2.cloned.1.call-update) | async-done | bytes 3145744 | tf_op jit(solution)/shard_map/all_gather | solution.py:200
  71.8 184.3 %while.27 = (s32[]{:T(128)}, bf16[4,512,3,64]{1,3,2,0:T(8,128)(2,1)}, f32[4,3,512]{2,1,0:T(4,128)}, s32[4]{0:T(128)S(1)}, s32[4096]{0:T(1024)}, /*index=5*/s32[1...) while((s32[]{:T(128)}, ...), condition=%wide.region_5.6_spmd, body=%wide.region_2.5_spmd.sunk | while | flops 1751353856 | bytes 108675712 | solution.py:102
  105.2 12.1 fusion.193
  127.1 12.1 fusion.191
  151.2 12.1 fusion.193
  173.1 12.1 fusion.191
  197.1 12.1 fusion.193
  243.1 12.1 fusion.193
  262.8 68.4 %all-reduce.11.cloned.1.call-done = bf16[1,2048,768]{2,1,0:T(8,128)(2,1)} async-done(((bf16[1,2048,768]{2,1,0:T(8,128)(2,1)}), bf16[1,2048,768]{2,1,0:T(8,128)(2,1)}) %all-reduce.11.cloned.1.call-update) | async-done | bytes 3145744 | tf_op jit(solution)/shard_map/psum | solution.py:219
  353.9 68.6 %all-reduce.13.cloned.1.call-done = bf16[1,2048,768]{2,1,0:T(8,128)(2,1)} async-done(((bf16[1,2048,768]{2,1,0:T(8,128)(2,1)}), bf16[1,2048,768]{2,1,0:T(8,128)(2,1)}) %all-reduce.13.cloned.1.call-update) | async-done | bytes 3145744 | tf_op jit(solution)/shard_map/psum | solution.py:236
  445.2 377.5 %while.28 = (s32[]{:T(128)}, f32[4096,3,64]{0,2,1:T(8,128)}, f32[4096,3,64]{0,2,1:T(8,128)}, bf16[4,512,3,64]{1,3,2,0:T(8,128)(2,1)}, bf16[4,512,3,64]{1,3,2,0:T...) while((s32[]{:T(128)}, f32[4096,3,64]{0,2,1:T(8,128)}, ...), condition=%wide.region_15.16_spmd.clone, body=%wide.region_13.15_spmd.clone.sunk | while | flops 4190177792 | bytes 234558224 | solution.py:153
  453.9 13.3 fusion.205
  467.2 12.5 fusion.208
  479.8 18.3 %multiply_reduce_fusion.4 = (f32[3,512]{1,0:T(4,128)S(1)}, f32[3,512,4096]{2,1,0:T(8,128)}) fusion(f32[3,512,4096]{2,1,0:T(8,128)} %fusion.205, f32[3,512]{1,0:T(4,128)S(1)} %dynamic-slice_bitcast_fusion.2, pred[512,4096]{1,0:T(8,128)(4,1)S(1)} %fusion.206, bf16[4096,3,64]{0,2,1:T(8,128)(2,1)} %get-tuple-element.564, ...), kind=kOutput, calls=%fused_computation.25.clone.1 | convolution fusion | flops 836762112 | bytes 54210564 | tf_op jit(solution)/shard_map/while/body/eval_jaxpr/qhd,khd->hqk/dot_general | solution.py:128
  498.1 21.9 %multiply_convert_fusion.5 = bf16[3,512,4096]{2,1,0:T(8,128)(2,1)} fusion(f32[3,512,4096]{2,1,0:T(8,128)} %get-tuple-element.479, f32[3,512,4096]{2,1,0:T(8,128)} %fusion.205, f32[3,512]{1,0:T(4,128)S(1)} %get-tuple-element.480, f32[3,512]{1,0:T(4,128)S(1)} %dynamic-slice_bitcast_fusion.2, pred[512,4096]{1,0:T(8,128)(4,1)S(1)} %fusion.206), kind=kLoop, calls=%fused_computation.24.clone.1 | loop fusion | flops 37748736 | bytes 65024000 | tf_op jit(solution)/shard_map/while/body/eval_jaxpr/convert_element_type | solution.py:132
  546.7 13.3 fusion.205
  560.0 13.6 fusion.208
  573.6 18.3 %multiply_reduce_fusion.4 = (f32[3,512]{1,0:T(4,128)S(1)}, f32[3,512,4096]{2,1,0:T(8,128)}) fusion(f32[3,512,4096]{2,1,0:T(8,128)} %fusion.205, f32[3,512]{1,0:T(4,128)S(1)} %dynamic-slice_bitcast_fusion.2, pred[512,4096]{1,0:T(8,128)(4,1)S(1)} %fusion.206, bf16[4096,3,64]{0,2,1:T(8,128)(2,1)} %get-tuple-element.564, ...), kind=kOutput, calls=%fused_computation.25.clone.1 | convolution fusion | flops 836762112 | bytes 54210564 | tf_op jit(solution)/shard_map/while/body/eval_jaxpr/qhd,khd->hqk/dot_general | solution.py:128
  591.9 21.9 %multiply_convert_fusion.5 = bf16[3,512,4096]{2,1,0:T(8,128)(2,1)} fusion(f32[3,512,4096]{2,1,0:T(8,128)} %get-tuple-element.479, f32[3,512,4096]{2,1,0:T(8,128)} %fusion.205, f32[3,512]{1,0:T(4,128)S(1)} %get-tuple-element.480, f32[3,512]{1,0:T(4,128)S(1)} %dynamic-slice_bitcast_fusion.2, pred[512,4096]{1,0:T(8,128)(4,1)S(1)} %fusion.206), kind=kLoop, calls=%fused_computation.24.clone.1 | loop fusion | flops 37748736 | bytes 65024000 | tf_op jit(solution)/shard_map/while/body/eval_jaxpr/convert_element_type | solution.py:132
  641.5 13.3 fusion.205
  654.7 13.6 fusion.208
  668.4 18.3 %multiply_reduce_fusion.4 = (f32[3,512]{1,0:T(4,128)S(1)}, f32[3,512,4096]{2,1,0:T(8,128)}) fusion(f32[3,512,4096]{2,1,0:T(8,128)} %fusion.205, f32[3,512]{1,0:T(4,128)S(1)} %dynamic-slice_bitcast_fusion.2, pred[512,4096]{1,0:T(8,128)(4,1)S(1)} %fusion.206, bf16[4096,3,64]{0,2,1:T(8,128)(2,1)} %get-tuple-element.564, ...), kind=kOutput, calls=%fused_computation.25.clone.1 | convolution fusion | flops 836762112 | bytes 54210564 | tf_op jit(solution)/shard_map/while/body/eval_jaxpr/qhd,khd->hqk/dot_general | solution.py:128
  686.7 21.9 %multiply_convert_fusion.5 = bf16[3,512,4096]{2,1,0:T(8,128)(2,1)} fusion(f32[3,512,4096]{2,1,0:T(8,128)} %get-tuple-element.479, f32[3,512,4096]{2,1,0:T(8,128)} %fusion.205, f32[3,512]{1,0:T(4,128)S(1)} %get-tuple-element.480, f32[3,512]{1,0:T(4,128)S(1)} %dynamic-slice_bitcast_fusion.2, pred[512,4096]{1,0:T(8,128)(4,1)S(1)} %fusion.206), kind=kLoop, calls=%fused_computation.24.clone.1 | loop fusion | flops 37748736 | bytes 65024000 | tf_op jit(solution)/shard_map/while/body/eval_jaxpr/convert_element_type | solution.py:132
  736.2 13.3 fusion.205
  749.5 13.6 fusion.208
  763.1 18.3 %multiply_reduce_fusion.4 = (f32[3,512]{1,0:T(4,128)S(1)}, f32[3,512,4096]{2,1,0:T(8,128)}) fusion(f32[3,512,4096]{2,1,0:T(8,128)} %fusion.205, f32[3,512]{1,0:T(4,128)S(1)} %dynamic-slice_bitcast_fusion.2, pred[512,4096]{1,0:T(8,128)(4,1)S(1)} %fusion.206, bf16[4096,3,64]{0,2,1:T(8,128)(2,1)} %get-tuple-element.564, ...), kind=kOutput, calls=%fused_computation.25.clone.1 | convolution fusion | flops 836762112 | bytes 54210564 | tf_op jit(solution)/shard_map/while/body/eval_jaxpr/qhd,khd->hqk/dot_general | solution.py:128
  781.4 21.9 %multiply_convert_fusion.5 = bf16[3,512,4096]{2,1,0:T(8,128)(2,1)} fusion(f32[3,512,4096]{2,1,0:T(8,128)} %get-tuple-element.479, f32[3,512,4096]{2,1,0:T(8,128)} %fusion.205, f32[3,512]{1,0:T(4,128)S(1)} %get-tuple-element.480, f32[3,512]{1,0:T(4,128)S(1)} %dynamic-slice_bitcast_fusion.2, pred[512,4096]{1,0:T(8,128)(4,1)S(1)} %fusion.206), kind=kLoop, calls=%fused_computation.24.clone.1 | loop fusion | flops 37748736 | bytes 65024000 | tf_op jit(solution)/shard_map/while/body/eval_jaxpr/convert_element_type | solution.py:132
  847.4 25.2 %reduce-scatter.2.cloned.1.call-done = bf16[1,2048,384]{1,2,0:T(8,128)(2,1)} async-done(((bf16[1,4096,384]{1,2,0:T(8,128)(2,1)}), bf16[1,2048,384]{1,2,0:T(8,128)(2,1)}) %reduce-scatter.2.cloned.1.call-update) | async-done | bytes 1572880 | tf_op jit(solution)/shard_map/reduce_scatter | solution.py:257
  894.0 157.1 %all-reduce.17.cloned.1.call-done = (f32[3,768,192]{1,2,0:T(8,128)}, f32[192,768]{1,0:T(8,128)}, f32[768,768]{1,0:T(8,128)}, f32[768,768]{1,0:T(8,128)}) async-done(((f32[3,768,192]{1,2,0:T(8,128)}, f32[192,768]{1,0:T(8,128)}, f32[768,768]{1,0:T(8,128)}, f32[768,768]{1,0:T(8,128)}), (f32[3,768,192]{1,2,0:T(8,128)}, f32[192,768]{1,0:T(8,128)}, f32[768,768]{1,0:T(8,128)}, ...) | async-done | bytes 7077904 | tf_op jit(solution)/shard_map/psum | solution.py:277
  1053.0 120.3 %all-reduce.19.cloned.1.call-done = (bf16[1,2048,768]{2,1,0:T(8,128)(2,1)}, bf16[1,2048,768]{2,1,0:T(8,128)(2,1)}) async-done(((bf16[1,2048,768]{2,1,0:T(8,128)(2,1)}, bf16[1,2048,768]{2,1,0:T(8,128)(2,1)}), (bf16[1,2048,768]{2,1,0:T(8,128)(2,1)}, bf16[1,2048,768]{2,1,0:T(8,128)(2,1)})) %all-reduce.19.cloned.1.call-update) | async-done | bytes 6291472 | tf_op jit(solution)/shard_map/psum | solution.py:228
  1194.5 24.2 %all-reduce = (f32[768]{0:T(1024)}, f32[768]{0:T(1024)}, f32[768]{0:T(1024)}, f32[2,192]{1,0:T(2,128)}, f32[768]{0:T(1024)}, /*index=5*/f32[768]{0:T(1024)}, f32[768]{0:T(1024)}, f32[768]{0:T(1024)}, f32[768]{0:T(1024)}) all-reduce(f32[768]{0:T(1024)S(1)} %get-tuple-element.297, ...), channel_id=1, replica_groups=mesh['dp'=4,'seq'=2,'tensor'=4] {'dp'}, use_global_device_ids=true, to_apply=%region_22.23 | all-reduce | flops 6528 | bytes 52224 | tf_op jit(solution)/shard_map/psum | solution.py:276
  1223.4 203.5 %all-reduce.15.cloned.1.call-done = (f32[3,768,192]{1,2,0:T(8,128)}, f32[192,768]{1,0:T(8,128)}, f32[768,768]{1,0:T(8,128)}, f32[768,768]{1,0:T(8,128)}) async-done(((f32[3,768,192]{1,2,0:T(8,128)}, f32[192,768]{1,0:T(8,128)}, f32[768,768]{1,0:T(8,128)}, f32[768,768]{1,0:T(8,128)}), (f32[3,768,192]{1,2,0:T(8,128)}, f32[192,768]{1,0:T(8,128)}, f32[768,768]{1,0:T(8,128)}, ...) | async-done | bytes 7077904 | tf_op jit(solution)/shard_map/psum | solution.py:276
  (317 shorter events, 358.6 us)
Async XLA Ops:
  7.2 334.1 %copy-start = (bf16[768,768]{1,0:T(8,128)(2,1)S(1)}, bf16[768,768]{1,0:T(8,128)(2,1)}, u32[]{:S(2)}) copy-start(bf16[768,768]{1,0:T(8,128)(2,1)} %param.33) | copy-start | bytes 3538948
  7.2 60.3 %all-gather.2.cloned.1.call-start = ((), (), s32[]{:S(2)}) async-start(), calls=%async_computation.1 | async-start | bytes 4718592 | tf_op jit(solution)/shard_map/all_gather | solution.py:200
  19.8 311.5 %all-reduce.11.cloned.1.call-start = ((), (), s32[]{:S(2)}) async-start(), calls=%async_computation.2 | async-start | bytes 6291456 | tf_op jit(solution)/shard_map/psum | solution.py:219
  81.1 12.1 copy-start.8
  93.2 12.0 copy-start.7
  93.2 12.0 copy-start.23
  127.1 12.1 copy-start.8
  139.2 12.0 copy-start.7
  139.2 12.0 copy-start.23
  173.1 12.1 copy-start.8
  185.1 12.0 copy-start.7
  185.1 12.0 copy-start.23
  219.0 12.1 copy-start.8
  231.1 12.0 copy-start.7
  231.1 12.0 copy-start.23
  256.1 79.3 %copy-start.55 = (s32[4]{0:T(128)}, s32[4]{0:T(128)S(1)}, u32[]{:S(2)}) copy-start(s32[4]{0:T(128)S(1)} %get-tuple-element.649) | copy-start | bytes 52
  256.1 79.3 %copy-start.58 = (bf16[13,13]{1,0:T(8,128)(2,1)}, bf16[13,13]{1,0:T(8,128)(2,1)S(1)}, u32[]{:S(2)}) copy-start(bf16[13,13]{1,0:T(8,128)(2,1)S(1)} %get-tuple-element.667) | copy-start | bytes 1018
  256.1 75.2 %copy-start.34 = (f32[768]{0:T(1024)S(1)}, f32[768]{0:T(1024)}, u32[]{:S(2)}) copy-start(f32[768]{0:T(1024)} %param.22) | copy-start | bytes 9220
  256.1 75.2 %copy-start.46 = (f32[768]{0:T(1024)S(1)}, f32[768]{0:T(1024)}, u32[]{:S(2)}) copy-start(f32[768]{0:T(1024)} %param.28) | copy-start | bytes 9220
  262.6 159.9 %all-reduce.13.cloned.1.call-start = ((), (), s32[]{:S(2)}) async-start(), calls=%async_computation.3 | async-start | bytes 6291456 | tf_op jit(solution)/shard_map/psum | solution.py:236
  353.8 518.8 %reduce-scatter.2.cloned.1.call-start = ((), (), s32[]{:S(2)}) async-start(), calls=%async_computation.4 | async-start | bytes 4718592 | tf_op jit(solution)/shard_map/reduce_scatter | solution.py:257
  434.5 10.8 copy-start.56
  829.0 222.2 %all-reduce.17.cloned.1.call-start = ((), (), s32[]{:S(2)}) async-start(), calls=%async_computation.6 | async-start | bytes 14155776 | tf_op jit(solution)/shard_map/psum | solution.py:277
  829.0 16.7 %slice-start = ((s8[6291456]{0:T(1024)(128)(4,1)}), s8[4194304]{0:T(1024)(128)(4,1)S(1)}, s32[]{:S(2)}) async-start(s8[6291456]{0:T(1024)(128)(4,1)} %bitcast.206), calls=%async_computation.8 | async-start | bytes 8388608
  879.8 293.5 %all-reduce.19.cloned.1.call-start = ((), (), s32[]{:S(2)}) async-start(), calls=%async_computation.7 | async-start | bytes 12582912 | tf_op jit(solution)/shard_map/psum | solution.py:228
  893.9 157.3 %copy-start.17 = (bf16[4,512,3,64]{1,3,2,0:T(8,128)(2,1)S(1)}, bf16[4,512,3,64]{1,3,2,0:T(8,128)(2,1)}, u32[]{:S(2)}) copy-start(bf16[4,512,3,64]{1,3,2,0:T(8,128)(2,1)} %get-tuple-element.653) | copy-start | bytes 2359300
  893.9 279.3 %copy-start.32 = (f32[2048]{0:T(1024)S(1)}, f32[2048]{0:T(1024)}, u32[]{:S(2)}) copy-start(f32[2048]{0:T(1024)} %copy-done.31) | copy-start | bytes 24580
  893.9 279.3 %copy-start.35 = (f32[768]{0:T(1024)S(1)}, f32[768]{0:T(1024)}, u32[]{:S(2)}) copy-start(f32[768]{0:T(1024)} %param.22) | copy-start | bytes 9220
  893.9 279.3 %copy-start.41 = (f32[768]{0:T(1024)S(1)}, f32[768]{0:T(1024)}, u32[]{:S(2)}) copy-start(f32[768]{0:T(1024)} %param.23) | copy-start | bytes 9220
  894.0 533.0 %all-reduce.15.cloned.1.call-start = ((), (), s32[]{:S(2)}) async-start(), calls=%async_computation.5 | async-start | bytes 14155776 | tf_op jit(solution)/shard_map/psum | solution.py:276
  1052.0 126.7 %copy-start.37 = (f32[2048]{0:T(1024)S(1)}, f32[2048]{0:T(1024)}, u32[]{:S(2)}) copy-start(f32[2048]{0:T(1024)} %copy-done.36) | copy-start | bytes 24580
  1178.7 42.0 %copy-start.48 = (f32[768]{0:T(1024)S(1)}, f32[768]{0:T(1024)}, u32[]{:S(2)}) copy-start(f32[768]{0:T(1024)} %param.34) | copy-start | bytes 9220
  (65 other events, 365.3 us)
Sparse Core Ops, SparseCore 0:
  19.9 47.6 all-gather.1
  262.7 68.4 all-reduce.10
  353.9 68.5 all-reduce.12
  829.1 43.4 reduce-scatter.1
  879.9 171.2 all-reduce.16
  1053.4 119.7 all-reduce.18
  1175.9 251.0 all-reduce.14
